TPU v7x, 32 devices: a whole 2x2x4 slice. The times are simulated.
32 devices in a mesh: band: 16 (over z, x, core), lev: 2 (over y).
Axes of the slice: x: 2, y: 2, z: 4, core: 2. Of those that a mesh axis runs over, the one named last changes fastest.
Arguments:
- field_grid: float32 [3, 8, 384, 2, 1536], P(None, 'lev', 'band'), may hold values from -6 to 6
- increment: float32 [3, 8, 384, 2, 1536], P(None, 'lev', 'band'), may hold values from -6 to 6
- points: int32 [384], P('band'), may hold values from 16 to 1536, as said below
- weights: float32 [384], replicated, may hold values from 0.0013020834 to 0.0052083335
- pair_slot: int32 [384], replicated, may hold values from 0 to 383, each once
- legendre: float32 [384, 384, 769], P(('band', 'lev')), may hold values from -6 to 6
- strength: float32 [3, 8], replicated, may hold values from 1 to 16
Outputs:
- stepped: float32 [3, 8, 384, 2, 1536], P(None, 'lev', 'band')
Inputs may be any that keep to these rules, and one draw needn't show every extreme that they name: points[j] lies within 32 of 16 + 1520 * j // 383, kept within 16 to 1536; the last latitude pair has 1536 cells. `pair_slot`: A permutation of 0 to 383; slot s is held by the device of joint band+lev index s // 12, at place s % 12, which holds legendre[s].
All inputs are finite; a program needn't handle non-finite values.
Results may differ from a plain program's by a relative error of at most 0.0003.
Values sent between devices are 32-bit elements; how exact they have to be, the bound alone decides.
A program may use at most 320 MiB of HBM per device.

v0:
```python
import math
import jax
import jax.numpy as jnp
from jax import lax
from jax.sharding import PartitionSpec as P

TWO_PI = 2.0 * math.pi


def dft_tables(counts, length, wavecount):
    inner = 32
    outer = length // inner
    orders = lax.iota(jnp.int32, wavecount)
    coarse = lax.iota(jnp.int32, outer) * inner
    finer = lax.iota(jnp.int32, inner)
    modulus = counts[:, None, None]
    step_angle = (TWO_PI / counts.astype(jnp.float32))[:, None, None]
    coarse_angle = (coarse[None, :, None] * orders[None, None, :] % modulus).astype(
        jnp.float32
    ) * step_angle
    finer_angle = (finer[None, :, None] * orders[None, None, :] % modulus).astype(
        jnp.float32
    ) * step_angle
    coarse_cos = jnp.cos(coarse_angle)[:, :, None, :]
    coarse_sin = jnp.sin(coarse_angle)[:, :, None, :]
    finer_cos = jnp.cos(finer_angle)[:, None, :, :]
    finer_sin = jnp.sin(finer_angle)[:, None, :, :]
    pair_count = counts.shape[0]
    full_cos = (coarse_cos * finer_cos - coarse_sin * finer_sin).reshape(
        pair_count, length, wavecount
    )
    full_sin = (coarse_sin * finer_cos + coarse_cos * finer_sin).reshape(
        pair_count, length, wavecount
    )
    places = lax.iota(jnp.int32, length)
    live = (places[None, :, None] < modulus) & (orders[None, None, :] <= (modulus - 1) // 2)
    cosines = jnp.where(live, full_cos, 0.0)
    sines = jnp.where(live, -full_sin, 0.0)
    return jnp.concatenate([cosines, sines], axis=2)


def body(field_grid, increment, points, weights, pair_slot, legendre, strength):
    band_count = lax.axis_size("band")
    level_groups = lax.axis_size("lev")
    summed = field_grid + increment
    fields = summed.shape[0]
    local_levels = summed.shape[1]
    band_pairs = summed.shape[2]
    length = summed.shape[4]
    wavecount = length // 2
    pair_total = wavecount // 2
    total_levels = local_levels * level_groups
    regrouped = lax.all_to_all(summed, "lev", split_axis=2, concat_axis=1, tiled=True)
    piece_pairs = band_pairs // level_groups
    counts = lax.dynamic_slice_in_dim(points, lax.axis_index("lev") * piece_pairs, piece_pairs)
    tables = dft_tables(counts, length, wavecount)
    row_count = fields * total_levels * 2
    pair_rows = jnp.moveaxis(regrouped, 2, 0).reshape(piece_pairs, row_count, length)
    spectra = jnp.einsum("pqx,pxk->pqk", pair_rows, tables, precision=lax.Precision.HIGHEST)
    spectra = spectra / counts.astype(jnp.float32)[:, None, None]
    piece_width = 2 * row_count
    by_wave = jnp.transpose(spectra.reshape(piece_pairs, row_count, 2, wavecount), (3, 0, 2, 1))
    by_wave = by_wave.reshape(wavecount, piece_pairs, piece_width)
    slot_ranks = lax.iota(jnp.int32, pair_total)
    pair_of_slot = jnp.zeros((pair_total,), jnp.int32).at[pair_slot].set(slot_ranks)
    wave_order = jnp.stack([pair_of_slot, wavecount - 1 - pair_of_slot], axis=1).reshape(wavecount)
    outgoing = jnp.take(by_wave, wave_order, axis=0)
    slot_count = legendre.shape[0]
    arrived = lax.all_to_all(outgoing, ("band", "lev"), split_axis=0, concat_axis=1, tiled=True)
    arrived = arrived.reshape(2 * slot_count, band_count, level_groups, piece_pairs, piece_width)
    row_width = 4 * fields * total_levels
    arrived = arrived.reshape(2 * slot_count, pair_total, row_width)
    lat_count = arrived.shape[1]
    own_slots = lax.axis_index(("band", "lev")) * slot_count + lax.iota(jnp.int32, slot_count)
    lower_wave = jnp.take(pair_of_slot, own_slots)
    columns = lax.iota(jnp.int32, wavecount + 1)
    second_member = columns[None, :] >= (wavecount - lower_wave)[:, None]
    degree = jnp.where(second_member, columns[None, :] - 1, lower_wave[:, None] + columns[None, :])
    wave_of_column = jnp.where(
        second_member, wavecount - 1 - lower_wave[:, None], lower_wave[:, None]
    )
    parity = jnp.where((degree - wave_of_column) % 2 == 0, 1.0, -1.0)
    weighted = arrived.reshape(slot_count, 2, lat_count, row_width) * weights[None, None, :, None]
    analysed = jnp.einsum("sjc,sejr->scer", legendre, weighted, precision=lax.Precision.HIGHEST)
    analysed = analysed.reshape(slot_count, wavecount + 1, 2, 2, fields * total_levels, 2)
    chosen = jnp.where(second_member[:, :, None, None, None], analysed[:, :, 1], analysed[:, :, 0])
    coefficients = chosen[..., 0] + parity[:, :, None, None] * chosen[..., 1]
    degree_real = degree.astype(jnp.float32)
    degree_ratio = degree_real * (degree_real + 1.0) / float((wavecount - 1) * wavecount)
    damping_rate = strength.reshape(fields * total_levels)
    damping = 1.0 / (1.0 + damping_rate[None, None, :] * (degree_ratio * degree_ratio)[:, :, None])
    damped = coefficients * damping[:, :, None, :]
    second_real = jnp.where(second_member, 1.0, 0.0)
    member_mask = jnp.stack([1.0 - second_real, second_real], axis=2)
    hemisphere_sign = jnp.stack([jnp.ones_like(parity), parity], axis=2)
    spread = damped[:, :, None, :, :, None] * member_mask[:, :, :, None, None, None]
    spread = spread * hemisphere_sign[:, :, None, None, None, :]
    spread = spread.reshape(slot_count, wavecount + 1, 2 * row_width)
    returned = jnp.einsum("sjc,scr->sjr", legendre, spread, precision=lax.Precision.HIGHEST)
    leaving = jnp.transpose(returned.reshape(slot_count, lat_count, 2, row_width), (0, 2, 1, 3))
    leaving = leaving.reshape(2 * slot_count, lat_count, row_width)
    leaving = leaving.reshape(2 * slot_count, band_count, level_groups, piece_pairs, piece_width)
    flat_back = leaving.reshape(2 * slot_count, band_count * level_groups, piece_pairs, piece_width)
    home_rows = lax.all_to_all(flat_back, ("band", "lev"), split_axis=1, concat_axis=0, tiled=True)
    home_rows = home_rows.reshape(wavecount, piece_pairs, piece_width)
    positions = (
        jnp.zeros((wavecount,), jnp.int32).at[wave_order].set(lax.iota(jnp.int32, wavecount))
    )
    restored = jnp.take(home_rows, positions, axis=0)
    spectral_rows = jnp.transpose(
        restored.reshape(wavecount, piece_pairs, 2, row_count), (1, 3, 2, 0)
    )
    spectral_rows = spectral_rows.reshape(piece_pairs, row_count, 2 * wavecount)
    doubling = jnp.where(lax.iota(jnp.int32, 2 * wavecount) % wavecount == 0, 1.0, 2.0)
    grid_rows = jnp.einsum(
        "pqk,pxk->pqx",
        spectral_rows * doubling[None, None, :],
        tables,
        precision=lax.Precision.HIGHEST,
    )
    grid_rows = jnp.moveaxis(grid_rows.reshape(piece_pairs, fields, total_levels, 2, length), 0, 2)
    return lax.all_to_all(grid_rows, "lev", split_axis=1, concat_axis=2, tiled=True)


def solution(mesh):
    return jax.shard_map(
        body,
        mesh=mesh,
        in_specs=(
            P(None, "lev", "band", None, None),
            P(None, "lev", "band", None, None),
            P("band"),
            P(),
            P(),
            P(("band", "lev"), None, None),
            P(),
        ),
        out_specs=P(None, "lev", "band", None, None),
        check_vma=False,
    )
```

profile of v0, /device:TPU:0, one launch (start us, length us, event | category | flops | bytes accessed | tf_op | source)
XLA Modules:
  0.0 824.1 jit_solution(12581593312345706289)
XLA Ops:
  0.0 7.1 copy_add_fusion
  7.1 4.4 all-to-all-start
  11.5 0.6 fusion.46
  12.3 23.5 %fusion.17 = (f32[12,48,768]{2,1,0:T(8,128)S(1)}, f32[12,48,768]{2,1,0:T(8,128)S(1)}) fusion(f32[12]{0:T(128)S(1)} %broadcast_divide_fusion.1, s32[12]{0:T(128)S(1)} %get-tuple-element.26, s32[48,768]{1,0:T(8,128)S(1)} %iota_multiply_fusion, pred[12]{0:T(512)(128)(4,1)S(1)} %broadcast_compare_fusion), kind=kLoop, calls=%fused_computation.43 | loop fusion | flops 3981312 | bytes 3686508 | tf_op jit(solution)/shard_map/cos | solution.py:24
  35.8 16.5 %fusion.24 = (f32[12,32,768]{2,1,0:T(8,128)S(1)}, f32[12,32,768]{2,1,0:T(8,128)}) fusion(f32[12]{0:T(128)S(1)} %broadcast_divide_fusion.1, s32[12]{0:T(128)S(1)} %get-tuple-element.26, s32[32,768]{1,0:T(8,128)S(1)} %iota_multiply_fusion.1, pred[12]{0:T(512)(128)(4,1)S(1)} %broadcast_compare_fusion), kind=kLoop, calls=%fused_computation.51 | loop fusion | flops 2654208 | bytes 2457708 | tf_op jit(solution)/shard_map/cos | solution.py:26
  52.3 37.0 %multiply_subtract_fusion = (f32[12,48,32,768]{3,2,1,0:T(8,128)}, f32[12,48,32,768]{3,2,1,0:T(8,128)}) fusion(f32[12,32,768]{2,1,0:T(8,128)} %get-tuple-element.17, f32[12,48,768]{2,1,0:T(8,128)S(1)} %get-tuple-element.15, f32[12,32,768]{2,1,0:T(8,128)S(1)} %get-tuple-element.16, f32[12,48,768]{2,1,0:T(8,128)S(1)} %get-tuple-element.14), kind=kLoop, calls=%fused_computation.11 | loop fusion | flops 99090432 | bytes 119144448 | tf_op jit(solution)/shard_map/sub | solution.py:29
  89.3 73.0 %and_select_fusion.1 = (f32[12,1536,768]{2,1,0:T(8,128)}, f32[12,1536,768]{2,1,0:T(8,128)}) fusion(f32[12,48,32,768]{3,2,1,0:T(8,128)} %get-tuple-element.10, pred[12,768]{1,0:T(8,128)(4,1)S(1)} %iota_compare_fusion.2, pred[12,1536]{1,0:T(8,128)(4,1)S(1)} %iota_compare_fusion, f32[12,48,32,768]{3,2,1,0:T(8,128)} %get-tuple-element.11), kind=kLoop, calls=%fused_computation.9 | loop fusion | flops 42467328 | bytes 226520064 | tf_op jit(solution)/shard_map/jit(_where)/select_n | solution.py:37
  162.3 3.3 scatter_custom_fusion
  165.7 0.8 copy.41
  166.5 1.1 reshape.699
  167.6 3.2 copy.45
  170.8 4.2 reshape.696
  175.1 74.6 %broadcast_divide_fusion = f32[12,48,1536]{2,1,0:T(8,128)} fusion(f32[12]{0:T(128)S(1)} %copy-done.5, f32[12,48,1536]{2,1,0:T(8,128)S(1)} %reshape.696, f32[12,1536,768]{2,1,0:T(8,128)} %get-tuple-element.19, f32[12,1536,768]{2,1,0:T(8,128)} %get-tuple-element.18), kind=kOutput, calls=%fused_computation.45 | convolution fusion | flops 16336650240 | bytes 120324144 | tf_op jit(solution)/shard_map/pqx,pxk->pqk/dot_general | solution.py:59
  249.6 2.4 copy.81
  252.0 4.2 copy.47
  256.2 6.6 gather_fusion.1
  262.8 7.8 broadcast_select_fusion.1
  270.7 7.9 all-to-all-start.1
  278.6 0.7 gather_fusion
  279.4 0.3 broadcast_subtract_fusion
  280.1 0.2 add_divide_fusion
  280.3 138.3 %all-to-all-done.1 = f32[768,12,96]{2,1,0:T(8,128)} async-done(((f32[768,12,96]{2,1,0:T(8,128)}), f32[768,12,96]{2,1,0:T(8,128)}, u32[]{:S(2)}, u32[]{:S(2)}) %all-to-all-start.1) | async-done | bytes 3538976 | tf_op jit(solution)/shard_map/all_to_all | solution.py:69
  418.6 4.7 copy.49
  423.4 1.7 broadcast_multiply_fusion.1
  425.1 34.2 %fusion.7 = f32[12,769,2,96]{1,3,2,0:T(8,128)} fusion(f32[12,384,769]{1,2,0:T(8,128)} %param.14, f32[12,2,384,96]{3,1,0,2:T(2,128)S(1)} %broadcast_multiply_fusion.1), kind=kOutput, calls=%fused_computation.27 | convolution fusion | flops 8164343808 | bytes 24800256 | tf_op jit(solution)/shard_map/sjc,sejr->scer/dot_general | solution.py:84
  459.3 10.5 %reshape.700 = f32[12,769,2,2,24,2]{1,5,4,3,2,0:T(2,128)} reshape(f32[12,769,2,96]{1,3,2,0:T(8,128)} %fusion.7) | data formatting | bytes 14174208 | tf_op jit(solution)/shard_map/reshape | solution.py:85
  469.8 5.6 fusion.5
  475.4 3.2 fusion.47
  478.6 0.3 fusion.13
  478.9 0.4 broadcast_multiply_fusion.2
  479.4 4.5 broadcast_multiply_fusion
  483.8 10.7 %mul.286 = f32[12,769,192]{1,2,0:T(8,128)} reshape(f32[12,769,2,2,24,2]{1,5,4,3,2,0:T(2,128)} %broadcast_multiply_fusion) | data formatting | bytes 14174208 | tf_op jit(solution)/shard_map/mul | solution.py:97
  494.6 19.0 %fusion.48 = f32[12,192,384]{2,1,0:T(8,128)S(1)} fusion(f32[12,769,192]{1,2,0:T(8,128)} %mul.286, f32[12,384,769]{1,2,0:T(8,128)} %param.14), kind=kOutput, calls=%fused_computation.120 | convolution fusion | flops 8164343808 | bytes 24800256 | tf_op jit(solution)/shard_map/sjc,scr->sjr/dot_general | solution.py:99
  513.6 5.5 copy.53
  519.0 3.7 all-to-all-start.2
  522.9 3.4 scatter_custom_fusion.1
  526.4 102.2 %all-to-all-done.2 = f32[24,32,12,96]{3,0,2,1:T(8,128)} async-done(((f32[24,32,12,96]{3,0,2,1:T(8,128)}), f32[24,32,12,96]{3,0,2,1:T(8,128)}, u32[]{:S(2)}, u32[]{:S(2)}) %all-to-all-start.2) | async-done | bytes 3538976 | tf_op jit(solution)/shard_map/all_to_all | solution.py:104
  628.6 2.7 copy.54
  631.4 5.4 copy.55
  636.8 6.6 gather_fusion.2
  643.4 8.0 broadcast_select_fusion
  651.4 5.9 copy.56
  657.3 2.4 copy.66
  659.8 112.1 %fusion = f32[12,48,1536]{2,1,0:T(8,128)} fusion(f32[12,1536,768]{2,1,0:T(8,128)} %get-tuple-element.19, f32[12,1536,768]{2,1,0:T(8,128)} %get-tuple-element.18, f32[12,48,1536]{2,1,0:T(8,128)S(1)} %bitcast.83, f32[1536]{0:T(1024)S(1)} %fusion.37), kind=kOutput, calls=%fused_computation.6 | convolution fusion | flops 16336650240 | bytes 120330240 | tf_op jit(solution)/shard_map/pqk,pxk->pqx/dot_general | solution.py:115
  771.9 4.0 reshape.706
  775.9 1.3 copy.82
  777.2 42.9 %all_to_all.66 = f32[3,8,12,2,1536]{4,3,0,2,1:T(2,128)S(1)} all-to-all(f32[3,8,12,2,1536]{4,3,0,2,1:T(2,128)S(1)} %bitcast.91), channel_id=1, replica_groups=mesh['band'=16,'lev'=2] {'lev'}, dimensions={1} | all-to-all | bytes 7077888 | tf_op jit(solution)/shard_map/all_to_all | solution.py:122
  820.2 3.7 copy.59
  (47 shorter events, 1.0 us)
Async XLA Ops:
  7.1 4.4 copy-start.4
  7.1 160.6 %all-to-all-start = ((f32[3,4,24,2,1536]{4,3,1,0,2:T(2,128)}), f32[3,4,24,2,1536]{4,3,1,0,2:T(2,128)S(1)}, u32[]{:S(2)}, u32[]{:S(2)}) async-start(f32[3,4,24,2,1536]{4,3,1,0,2:T(2,128)} %copy_add_fusion), calls=%async_computation | async-start | bytes 7077888 | tf_op jit(solution)/shard_map/all_to_all | solution.py:53
  89.3 73.0 %copy-start.3 = (s32[384]{0:T(512)S(1)}, s32[384]{0:T(512)}, u32[]{:S(2)}) copy-start(s32[384]{0:T(512)} %param.13) | copy-start | bytes 4612
  170.8 4.2 copy-start.5
  270.7 8.6 %copy-start.2 = (f32[3,8]{1,0:T(4,128)S(1)}, f32[3,8]{1,0:T(4,128)}, u32[]{:S(2)}) copy-start(f32[3,8]{1,0:T(4,128)} %param.15) | copy-start | bytes 292
  270.7 147.9 %all-to-all-start.1 = ((f32[768,12,96]{2,1,0:T(8,128)}), f32[768,12,96]{2,1,0:T(8,128)}, u32[]{:S(2)}, u32[]{:S(2)}) async-start(f32[768,12,96]{2,1,0:T(8,128)} %broadcast_select_fusion.1), calls=%async_computation.1 | async-start | bytes 12582912 | tf_op jit(solution)/shard_map/all_to_all | solution.py:69
  418.6 4.8 copy-start.1
  519.0 3.7 copy-start
  519.0 109.6 %all-to-all-start.2 = ((f32[24,32,12,96]{3,0,2,1:T(8,128)}), f32[24,32,12,96]{3,0,2,1:T(8,128)}, u32[]{:S(2)}, u32[]{:S(2)}) async-start(f32[24,32,12,96]{3,0,2,1:T(8,128)} %bitcast.84), calls=%async_computation.2 | async-start | bytes 9437184 | tf_op jit(solution)/shard_map/all_to_all | solution.py:104
where the time goes:
time: 835 us; the launch traced here: 824 us
  waiting for transfers between devices  241 us (29%)
  matrix products  240 us (29%)
  other arithmetic  187 us (22%)
  local copies, waits for them, and re-layouts  97 us (12%)
  blocking collectives  42.9 us (5%)
  starting transfers between devices  16 us (2%)
    all_to_all x1, waiting for transfers between devices, body(): lax.all_to_all(outgoing, ('band', 'lev'), split_axis=0, concat_axis=1, ti...  138 us
    dot_general x1, matrix products, body(): jnp.einsum('pqk,pxk->pqx', spectral_rows * doubling[None, None, :], table...  112 us
    all_to_all x1, waiting for transfers between devices, body(): lax.all_to_all(flat_back, ('band', 'lev'), split_axis=1, concat_axis=0, t...  102 us
    dot_general x1, matrix products, body(): jnp.einsum('pqx,pxk->pqk', pair_rows, tables, precision=lax.Precision.HIG...  74.6 us
    select_n x1, other arithmetic, dft_tables(): cosines = jnp.where(live, full_cos, 0.0)  73 us
    all_to_all x1, blocking collectives, body(): lax.all_to_all(grid_rows, 'lev', split_axis=1, concat_axis=2, tiled=True)  42.9 us
    sub x1, other arithmetic, dft_tables(): coarse_cos * finer_cos - coarse_sin * finer_sin  37 us
    dot_general x1, matrix products, body(): jnp.einsum('sjc,sejr->scer', legendre, weighted, precision=lax.Precision....  34.2 us
  transfers between devices with their start and end apart: 3, of which 2 were waited for; matrix products, arithmetic and copies ran while one was open for 20% of the time, Pallas kernels for 0%

commit v1 on v0

--- a/solution.py
+++ b/solution.py
@@ -66,7 +66,15 @@
     wave_order = jnp.stack([pair_of_slot, wavecount - 1 - pair_of_slot], axis=1).reshape(wavecount)
     outgoing = jnp.take(by_wave, wave_order, axis=0)
     slot_count = legendre.shape[0]
-    arrived = lax.all_to_all(outgoing, ("band", "lev"), split_axis=0, concat_axis=1, tiled=True)
+    arrived = jnp.concatenate(
+        lax.all_to_all(
+            jnp.stack(jnp.split(outgoing, lax.axis_size(("band", "lev")), axis=0)),
+            ("band", "lev"),
+            0,
+            0,
+        ),
+        axis=1,
+    )
     arrived = arrived.reshape(2 * slot_count, band_count, level_groups, piece_pairs, piece_width)
     row_width = 4 * fields * total_levels
     arrived = arrived.reshape(2 * slot_count, pair_total, row_width)

time: 835 us -> 807 us (0.966)
  waiting for transfers between devices: 241 us -> 210 us
    all_to_all x1, waiting for transfers between devices: 138 us -> 104 us  [body(): lax.all_to_all(jnp.stack(jnp.split(outgoing, lax.axis_size(('band', 'lev'...]
  transfers between devices with their start and end apart: 3 -> 3, of which waited for: 2 -> 2; matrix products, arithmetic and copies ran while one was open for 20% -> 21% of each run, Pallas kernels for 0% -> 0%
where the time goes in v1:
time: 807 us; the launch traced here: 796 us
  matrix products  240 us (30%)
  waiting for transfers between devices  210 us (26%)
  other arithmetic  188 us (23%)
  local copies, waits for them, and re-layouts  98.5 us (12%)
  blocking collectives  42.9 us (5%)
  starting transfers between devices  15.7 us (2%)
    dot_general x1, matrix products, body(): jnp.einsum('pqk,pxk->pqx', spectral_rows * doubling[None, None, :], table...  112 us
    all_to_all x1, waiting for transfers between devices, body(): lax.all_to_all(flat_back, ('band', 'lev'), split_axis=1, concat_axis=0, t...  106 us
    all_to_all x1, waiting for transfers between devices, body(): lax.all_to_all(jnp.stack(jnp.split(outgoing, lax.axis_size(('band', 'lev'...  104 us
    dot_general x1, matrix products, body(): jnp.einsum('pqx,pxk->pqk', pair_rows, tables, precision=lax.Precision.HIG...  74.6 us
    select_n x1, other arithmetic, dft_tables(): cosines = jnp.where(live, full_cos, 0.0)  72.9 us
    all_to_all x1, blocking collectives, body(): lax.all_to_all(grid_rows, 'lev', split_axis=1, concat_axis=2, tiled=True)  42.9 us
    sub x1, other arithmetic, dft_tables(): coarse_cos * finer_cos - coarse_sin * finer_sin  37 us
    dot_general x1, matrix products, body(): jnp.einsum('sjc,sejr->scer', legendre, weighted, precision=lax.Precision....  34.6 us
  transfers between devices with their start and end apart: 3, of which 2 were waited for; matrix products, arithmetic and copies ran while one was open for 21% of the time, Pallas kernels for 0%

profile of v1, /device:TPU:0, one launch (start us, length us, event | category | flops | bytes accessed | tf_op | source)
XLA Modules:
  0.0 795.7 jit_solution(6864536886623114751)
XLA Ops:
  0.0 7.1 copy_add_fusion
  7.1 4.3 all-to-all-start
  11.3 0.6 fusion.78
  12.2 23.8 %fusion.17 = (f32[12,48,768]{2,1,0:T(8,128)S(1)}, f32[12,48,768]{2,1,0:T(8,128)S(1)}) fusion(f32[12]{0:T(128)S(1)} %broadcast_divide_fusion.1, s32[12]{0:T(128)S(1)} %get-tuple-element.26, s32[48,768]{1,0:T(8,128)S(1)} %iota_multiply_fusion, pred[12]{0:T(512)(128)(4,1)S(1)} %broadcast_compare_fusion), kind=kLoop, calls=%fused_computation.43 | loop fusion | flops 3981312 | bytes 3686508 | tf_op jit(solution)/shard_map/cos | solution.py:24
  35.9 16.5 %fusion.24 = (f32[12,32,768]{2,1,0:T(8,128)S(1)}, f32[12,32,768]{2,1,0:T(8,128)}) fusion(f32[12]{0:T(128)S(1)} %broadcast_divide_fusion.1, s32[12]{0:T(128)S(1)} %get-tuple-element.26, s32[32,768]{1,0:T(8,128)S(1)} %iota_multiply_fusion.1, pred[12]{0:T(512)(128)(4,1)S(1)} %broadcast_compare_fusion), kind=kLoop, calls=%fused_computation.51 | loop fusion | flops 2654208 | bytes 2457708 | tf_op jit(solution)/shard_map/cos | solution.py:26
  52.5 37.0 %multiply_subtract_fusion = (f32[12,48,32,768]{3,2,1,0:T(8,128)}, f32[12,48,32,768]{3,2,1,0:T(8,128)}) fusion(f32[12,32,768]{2,1,0:T(8,128)} %get-tuple-element.17, f32[12,48,768]{2,1,0:T(8,128)S(1)} %get-tuple-element.15, f32[12,32,768]{2,1,0:T(8,128)S(1)} %get-tuple-element.16, f32[12,48,768]{2,1,0:T(8,128)S(1)} %get-tuple-element.14), kind=kLoop, calls=%fused_computation.11 | loop fusion | flops 99090432 | bytes 119144448 | tf_op jit(solution)/shard_map/sub | solution.py:29
  89.5 72.9 %and_select_fusion.1 = (f32[12,1536,768]{2,1,0:T(8,128)}, f32[12,1536,768]{2,1,0:T(8,128)}) fusion(f32[12,48,32,768]{3,2,1,0:T(8,128)} %get-tuple-element.10, pred[12,768]{1,0:T(8,128)(4,1)S(1)} %iota_compare_fusion.2, pred[12,1536]{1,0:T(8,128)(4,1)S(1)} %iota_compare_fusion, f32[12,48,32,768]{3,2,1,0:T(8,128)} %get-tuple-element.11), kind=kLoop, calls=%fused_computation.9 | loop fusion | flops 42467328 | bytes 226520064 | tf_op jit(solution)/shard_map/jit(_where)/select_n | solution.py:37
  162.4 2.9 scatter_custom_fusion
  165.4 0.8 copy.71
  166.2 1.1 reshape.706
  167.3 1.1 reshape.701
  168.4 0.6 iota.109
  169.0 3.7 scatter_custom_fusion.1
  172.8 0.6 pad_clamp_fusion
  173.3 0.5 compare_and_fusion.1
  173.9 3.2 copy.75
  177.1 4.2 reshape.698
  181.3 74.6 %broadcast_divide_fusion = f32[12,48,1536]{2,1,0:T(8,128)} fusion(f32[12]{0:T(128)S(1)} %copy-done.6, f32[12,48,1536]{2,1,0:T(8,128)S(1)} %reshape.698, f32[12,1536,768]{2,1,0:T(8,128)} %get-tuple-element.19, f32[12,1536,768]{2,1,0:T(8,128)} %get-tuple-element.18), kind=kOutput, calls=%fused_computation.45 | convolution fusion | flops 16336650240 | bytes 120324144 | tf_op jit(solution)/shard_map/pqx,pxk->pqk/dot_general | solution.py:59
  255.9 2.4 copy.109
  258.3 4.2 copy.77
  262.4 6.7 gather_fusion.1
  269.1 5.0 broadcast_select_fusion.1
  274.9 4.1 copy.78
  279.0 7.7 all-to-all-start.1
  286.7 0.7 gather_fusion
  288.4 103.9 %all-to-all-done.1 = f32[32,24,12,96]{3,1,2,0:T(8,128)} async-done(((f32[32,24,12,96]{3,1,2,0:T(8,128)}), f32[32,24,12,96]{3,1,2,0:T(8,128)}, u32[]{:S(2)}, u32[]{:S(2)}) %all-to-all-start.1) | async-done | bytes 3538976 | tf_op jit(solution)/shard_map/all_to_all | solution.py:70
  392.3 4.0 broadcast_multiply_fusion.1
  396.4 34.6 %fusion.7 = f32[12,769,2,96]{1,3,2,0:T(8,128)} fusion(f32[12,384,769]{1,2,0:T(8,128)} %param.14, f32[12,2,384,96]{3,1,0,2:T(2,128)S(1)} %broadcast_multiply_fusion.1), kind=kOutput, calls=%fused_computation.27 | convolution fusion | flops 8164343808 | bytes 24800256 | tf_op jit(solution)/shard_map/sjc,sejr->scer/dot_general | solution.py:92
  431.0 10.4 %reshape.703 = f32[12,769,2,2,24,2]{1,5,4,3,2,0:T(2,128)} reshape(f32[12,769,2,96]{1,3,2,0:T(8,128)} %fusion.7) | data formatting | bytes 14174208 | tf_op jit(solution)/shard_map/reshape | solution.py:93
  441.5 5.6 fusion.5
  447.1 3.2 fusion.79
  451.0 4.5 broadcast_multiply_fusion
  455.5 10.7 %mul.286 = f32[12,769,192]{1,2,0:T(8,128)} reshape(f32[12,769,2,2,24,2]{1,5,4,3,2,0:T(2,128)} %broadcast_multiply_fusion) | data formatting | bytes 14174208 | tf_op jit(solution)/shard_map/mul | solution.py:105
  466.2 18.6 %fusion.80 = f32[12,192,384]{2,1,0:T(8,128)S(1)} fusion(f32[12,769,192]{1,2,0:T(8,128)} %mul.286, f32[12,384,769]{1,2,0:T(8,128)} %param.14), kind=kOutput, calls=%fused_computation.184 | convolution fusion | flops 8164343808 | bytes 24800256 | tf_op jit(solution)/shard_map/sjc,scr->sjr/dot_general | solution.py:107
  484.8 5.4 copy.82
  490.2 3.8 all-to-all-start.2
  494.1 105.8 %all-to-all-done.2 = f32[24,32,12,96]{3,0,2,1:T(8,128)} async-done(((f32[24,32,12,96]{3,0,2,1:T(8,128)}), f32[24,32,12,96]{3,0,2,1:T(8,128)}, u32[]{:S(2)}, u32[]{:S(2)}) %all-to-all-start.2) | async-done | bytes 3538976 | tf_op jit(solution)/shard_map/all_to_all | solution.py:112
  599.8 2.7 copy.83
  602.6 5.4 copy.84
  608.0 6.7 gather_fusion.2
  614.6 7.8 broadcast_select_fusion
  622.5 5.9 copy.85
  628.4 2.4 copy.94
  630.9 112.1 %fusion = f32[12,48,1536]{2,1,0:T(8,128)} fusion(f32[12,1536,768]{2,1,0:T(8,128)} %get-tuple-element.19, f32[12,1536,768]{2,1,0:T(8,128)} %get-tuple-element.18, f32[12,48,1536]{2,1,0:T(8,128)S(1)} %bitcast.210, f32[1536]{0:T(1024)S(1)} %fusion.69), kind=kOutput, calls=%fused_computation.6 | convolution fusion | flops 16336650240 | bytes 120330240 | tf_op jit(solution)/shard_map/pqk,pxk->pqx/dot_general | solution.py:123
  742.9 4.3 reshape.709
  747.2 1.3 copy.110
  748.6 42.9 %all_to_all.56 = f32[3,8,12,2,1536]{4,3,0,2,1:T(2,128)S(1)} all-to-all(f32[3,8,12,2,1536]{4,3,0,2,1:T(2,128)S(1)} %bitcast.217), channel_id=1, replica_groups=mesh['band'=16,'lev'=2] {'lev'}, dimensions={1} | all-to-all | bytes 7077888 | tf_op jit(solution)/shard_map/all_to_all | solution.py:130
  791.5 3.7 copy.88
  (80 shorter events, 2.6 us)
Async XLA Ops:
  0.0 11.3 %copy-start.5 = (s32[24]{0:T(128)S(1)}, s32[24]{0:T(128)}, u32[]{:S(2)}) copy-start(s32[24]{0:T(128)} %param.11) | copy-start | bytes 292
  7.1 166.8 %all-to-all-start = ((f32[3,4,24,2,1536]{4,3,1,0,2:T(2,128)}), f32[3,4,24,2,1536]{4,3,1,0,2:T(2,128)S(1)}, u32[]{:S(2)}, u32[]{:S(2)}) async-start(f32[3,4,24,2,1536]{4,3,1,0,2:T(2,128)} %copy_add_fusion), calls=%async_computation | async-start | bytes 7077888 | tf_op jit(solution)/shard_map/all_to_all | solution.py:53
  89.5 73.0 %copy-start.4 = (s32[384]{0:T(512)S(1)}, s32[384]{0:T(512)}, u32[]{:S(2)}) copy-start(s32[384]{0:T(512)} %param.13) | copy-start | bytes 4612
  173.9 7.4 copy-start.6
  258.3 4.2 copy-start
  262.4 6.7 copy-start.1
  279.0 8.4 %copy-start.3 = (f32[3,8]{1,0:T(4,128)S(1)}, f32[3,8]{1,0:T(4,128)}, u32[]{:S(2)}) copy-start(f32[3,8]{1,0:T(4,128)} %param.15) | copy-start | bytes 292
  279.0 113.4 %copy-start.2 = (f32[384]{0:T(512)S(1)}, f32[384]{0:T(512)}, u32[]{:S(2)}) copy-start(f32[384]{0:T(512)} %param.12) | copy-start | bytes 4612
  279.0 113.4 %all-to-all-start.1 = ((f32[32,24,12,96]{3,1,2,0:T(8,128)}), f32[32,24,12,96]{3,1,2,0:T(8,128)}, u32[]{:S(2)}, u32[]{:S(2)}) async-start(f32[32,24,12,96]{3,1,2,0:T(8,128)} %copy.78), calls=%async_computation.1 | async-start | bytes 9437184 | tf_op jit(solution)/shard_map/all_to_all | solution.py:70
  490.2 109.6 %all-to-all-start.2 = ((f32[24,32,12,96]{3,0,2,1:T(8,128)}), f32[24,32,12,96]{3,0,2,1:T(8,128)}, u32[]{:S(2)}, u32[]{:S(2)}) async-start(f32[24,32,12,96]{3,0,2,1:T(8,128)} %bitcast.211), calls=%async_computation.2 | async-start | bytes 9437184 | tf_op jit(solution)/shard_map/all_to_all | solution.py:112
